TPU v7x, 32 devices: a whole 2x2x4 slice. The times are simulated.
32 devices in a mesh: gx: 8 (over z, core), gy: 4 (over y, x).
Axes of the slice: x: 2, y: 2, z: 4, core: 2. Of those that a mesh axis runs over, the one named last changes fastest.
Arguments:
- load: float32 [8, 4, 320, 768], P('gx', 'gy'), may hold values from -6 to 6
- stiffness: bfloat16 [8, 4, 768, 768], P('gx', 'gy'), may hold values from -0.5 to 3, as said below
- local_inverse: bfloat16 [8, 4, 768, 768], P('gx', 'gy'), may hold values from -0.5 to 3, as said below
- phi: float32 [8, 4, 8, 768], P('gx', 'gy'), may hold values from -2.5 to 2.5
- level2_inverse: float32 [8, 32, 32], P('gx'), may hold values from -0.5 to 3, as said below
- level3_inverse: bfloat16 [128, 128], replicated, may hold values from -0.5 to 3, as said below
- aggregate: int32 [8, 4], P('gx', 'gy'), may hold values from 0 to 1
Outputs:
- solution: float32 [8, 4, 320, 768], P('gx', 'gy')
Inputs may be any that keep to these rules, and one draw needn't show every extreme that they name: `stiffness`: every block is symmetric positive definite. `local_inverse`: every block is symmetric positive definite. `level2_inverse`: every block is symmetric positive definite. `level3_inverse`: symmetric positive definite.
All inputs are finite; a program needn't handle non-finite values.
Results may differ from a plain program's by a relative error of at most 0.0091.
Values may be sent and summed in bfloat16 or wider, within the bound.
A program may use at most 64 MiB of HBM per device.

v0:
```python
import jax
import jax.numpy as jnp
from jax import lax
from jax.sharding import PartitionSpec as P

NAGG = 2
ITERS = 2
HIGH = lax.Precision.HIGHEST


def from_behind(value, axis, steps):
    count = lax.axis_size(axis)
    first, last = (max(0, -steps), min(count, count - steps))
    return lax.ppermute(value, axis, [(source, source + steps) for source in range(first, last)])


def assemble(vec):
    rows, total = vec.shape
    width = total // 4
    edges = vec.reshape(rows, 4, width)
    west, east, south, north = (edges[:, 0], edges[:, 1], edges[:, 2], edges[:, 3])
    new_west = west + from_behind(east, "gx", 1)
    new_east = east + from_behind(west, "gx", -1)
    new_south = south + from_behind(north, "gy", 1)
    new_north = north + from_behind(south, "gy", -1)
    return jnp.stack([new_west, new_east, new_south, new_north], axis=1).reshape(rows, total)


def contract_last(left, right):
    return lax.dot_general(
        left, right, (((1,), (1,)), ((), ())), preferred_element_type=jnp.float32
    )


def contract_high(left, right):
    return lax.dot_general(
        left, right, (((1,), (1,)), ((), ())), precision=HIGH, preferred_element_type=jnp.float32
    )


def body(load, stiffness, local_inverse, phi, level2_inverse, level3_inverse, aggregate):
    load_here = load[0, 0]
    stiff = stiffness[0, 0]
    inverse = local_inverse[0, 0]
    basis = phi[0, 0]
    second_inv = level2_inverse[0]
    rows, total = load_here.shape
    width = total // 4
    primal_count = basis.shape[0]
    block = NAGG * primal_count
    col = lax.axis_index("gx")
    row = lax.axis_index("gy")
    cols_total = lax.axis_size("gx")
    rows_total = lax.axis_size("gy")
    edge_w = jnp.stack(
        [
            jnp.where(col > 0, 0.5, 1.0),
            jnp.where(col < cols_total - 1, 0.5, 1.0),
            jnp.where(row > 0, 0.5, 1.0),
            jnp.where(row < rows_total - 1, 0.5, 1.0),
        ]
    ).astype(jnp.float32)
    weights = jnp.repeat(edge_w, width)
    labels = jnp.arange(NAGG, dtype=jnp.int32)
    own_onehot = (aggregate[0, 0] == labels).astype(jnp.float32)
    members = lax.all_gather(aggregate[0], "gy", axis=0, tiled=True)
    group_onehot = (members[:, None] == labels[None, :]).astype(jnp.float32)

    def apply(vec):
        return assemble(contract_last(vec.astype(jnp.bfloat16), stiff))

    def precondition(resid):
        scaled = weights * resid
        local = contract_last(scaled.astype(jnp.bfloat16), inverse)
        primal = contract_high(scaled, basis)
        grouped = lax.all_gather(primal, "gy", axis=1, tiled=True)
        summed = jnp.einsum(
            "rbp,bq->rqp",
            grouped.reshape(rows, rows_total, primal_count),
            group_onehot,
            precision=HIGH,
        )
        summed = summed.reshape(rows, block)
        summed = summed.astype(jnp.bfloat16)
        second = contract_high(grouped, second_inv)
        second_own = lax.dynamic_slice_in_dim(second, row * primal_count, primal_count, 1)
        everyone = lax.all_gather(summed, "gx", axis=1, tiled=True)
        mine = lax.dynamic_slice_in_dim(level3_inverse, col * block, block, 0)
        third = contract_last(everyone, mine)
        third_own = jnp.einsum(
            "rqp,q->rp", third.reshape(rows, NAGG, primal_count), own_onehot, precision=HIGH
        )
        full = local + jnp.dot(
            second_own + third_own, basis, precision=HIGH, preferred_element_type=jnp.float32
        )
        return assemble(weights * full)

    def inner(left, right):
        return jnp.sum(weights * left * right, axis=1)

    rhs = assemble(load_here)
    solution = jnp.zeros_like(rhs)
    resid = rhs

    def paired(resid, zvec, wvec):
        return lax.psum((inner(resid, zvec), inner(zvec, wvec)), ("gx", "gy"))

    zvec = precondition(resid)
    wvec = apply(zvec)
    gamma, delta = paired(resid, zvec, wvec)
    alpha = gamma / delta
    pvec, svec = (zvec, wvec)
    for step in range(ITERS):
        solution = solution + alpha[:, None] * pvec
        resid = resid - alpha[:, None] * svec
        if step < ITERS - 1:
            zvec = precondition(resid)
            wvec = apply(zvec)
            newer, delta = paired(resid, zvec, wvec)
            beta = newer / gamma
            alpha = newer / (delta - beta * newer / alpha)
            pvec = zvec + beta[:, None] * pvec
            svec = wvec + beta[:, None] * svec
            gamma = newer
    return solution[None, None]


def solution(mesh):
    return jax.shard_map(
        body,
        mesh=mesh,
        in_specs=(
            P("gx", "gy", None, None),
            P("gx", "gy", None, None),
            P("gx", "gy", None, None),
            P("gx", "gy", None, None),
            P("gx", None, None),
            P(),
            P("gx", "gy"),
        ),
        out_specs=P("gx", "gy", None, None),
        check_vma=False,
    )
```

profile of v0, /device:TPU:0, one launch (start us, length us, event | category | flops | bytes accessed | tf_op | source)
XLA Modules:
  0.0 265.9 jit_solution(13401014235180399910)
XLA Ops:
  2.6 2.4 collective-permute-start
  5.0 4.2 %collective-permute-start.2 = (f32[320,192]{0,1:T(8,128)}, f32[320,192]{0,1:T(8,128)S(1)}, u32[]{:S(2)}, u32[]{:S(2)}) collective-permute-start(f32[320,192]{0,1:T(8,128)} %get-tuple-element.58), channel_id=1, source_target_pairs={{0,1},{1,2},{2,3},{4,5},{5,6},{6,7},{8,9},{9,10},{10,11},{12,13},{... | collective-permute-start | bytes 737288 | tf_op jit(solution)/shard_map/ppermute | solution.py:14
  13.8 12.4 %all-reduce = s32[4]{0:T(128)} all-reduce(s32[4]{0:T(128)S(1)} %bitcast_dynamic-update-slice_fusion), channel_id=2, replica_groups=mesh['gx'=8,'gy'=4] {'gy'}, use_global_device_ids=true, to_apply=%add | all-reduce | flops 4 | bytes 32
  30.1 9.1 %all_gather.15 = f32[320,32]{0,1:T(8,128)S(1)} all-gather(f32[320,8]{0,1:T(8,128)S(1)} %fusion.18), channel_id=1, replica_groups=mesh['gx'=8,'gy'=4] {'gy'}, dimensions={1}, use_global_device_ids=true | all-gather | bytes 51200 | tf_op jit(solution)/shard_map/all_gather | solution.py:76
  40.0 14.4 %all_gather.17 = bf16[320,128]{0,1:T(8,128)(2,1)S(1)} all-gather(bf16[320,16]{0,1:T(8,128)(2,1)S(1)} %bitcast.227), channel_id=1, replica_groups=mesh['gx'=8,'gy'=4] {'gx'}, dimensions={1}, use_global_device_ids=true | all-gather | bytes 92160 | tf_op jit(solution)/shard_map/all_gather | solution.py:87
  58.9 1.8 fusion.5
  60.7 1.9 fusion.1
  64.3 2.3 collective-permute-start.4
  66.6 1.9 collective-permute-start.6
  71.1 4.1 %collective-permute-done.6 = f32[320,192]{0,1:T(8,128)S(1)} collective-permute-done((f32[320,192]{0,1:T(8,128)S(1)}, f32[320,192]{0,1:T(8,128)S(1)}, u32[]{:S(2)}, u32[]{:S(2)}) %collective-permute-start.6) | collective-permute-done | bytes 245792 | tf_op jit(solution)/shard_map/ppermute | solution.py:14
  75.2 8.2 %collective-permute-done.7 = f32[320,192]{0,1:T(8,128)S(1)} collective-permute-done((f32[320,192]{0,1:T(8,128)S(1)}, f32[320,192]{0,1:T(8,128)S(1)}, u32[]{:S(2)}, u32[]{:S(2)}) %collective-permute-start.7) | collective-permute-done | bytes 245792 | tf_op jit(solution)/shard_map/ppermute | solution.py:14
  86.0 4.0 %collective-permute-start.10 = (f32[320,192]{0,1:T(8,128)S(1)}, f32[320,192]{0,1:T(8,128)S(1)}, u32[]{:S(2)}, u32[]{:S(2)}) collective-permute-start(f32[320,192]{0,1:T(8,128)S(1)} %get-tuple-element.42), channel_id=1, source_target_pairs={{0,1},{1,2},{2,3},{4,5},{5,6},{6,7},{8,9},{9,10},{10,11},{12,13},{... | collective-permute-start | bytes 737288 | tf_op jit(solution)/shard_map/ppermute | solution.py:14
  92.6 4.4 %collective-permute-done.10 = f32[320,192]{0,1:T(8,128)S(1)} collective-permute-done((f32[320,192]{0,1:T(8,128)S(1)}, f32[320,192]{0,1:T(8,128)S(1)}, u32[]{:S(2)}, u32[]{:S(2)}) %collective-permute-start.10) | collective-permute-done | bytes 245792 | tf_op jit(solution)/shard_map/ppermute | solution.py:14
  97.0 6.5 %collective-permute-done.11 = f32[320,192]{0,1:T(8,128)S(1)} collective-permute-done((f32[320,192]{0,1:T(8,128)S(1)}, f32[320,192]{0,1:T(8,128)S(1)}, u32[]{:S(2)}, u32[]{:S(2)}) %collective-permute-start.11) | collective-permute-done | bytes 245792 | tf_op jit(solution)/shard_map/ppermute | solution.py:14
  103.7 2.0 multiply_reduce_fusion.1
  105.7 39.3 %all-reduce.2 = (f32[320]{0:T(512)S(1)}, f32[320]{0:T(512)S(1)}) all-reduce(f32[320]{0:T(512)} %get-tuple-element.8, f32[320]{0:T(512)} %get-tuple-element.7), channel_id=1, replica_groups=mesh['gx'=8,'gy'=4] {'gx','gy'}, use_global_device_ids=true, to_apply=%region_1.2 | all-reduce | flops 640 | bytes 5120 | tf_op jit(solution)/shard_map/psum | solution.py:106
  145.7 2.4 fusion.42
  148.8 9.0 %all_gather.18 = f32[320,32]{0,1:T(8,128)S(1)} all-gather(f32[320,8]{0,1:T(8,128)S(1)} %fusion.15), channel_id=1, replica_groups=mesh['gx'=8,'gy'=4] {'gy'}, dimensions={1}, use_global_device_ids=true | all-gather | bytes 51200 | tf_op jit(solution)/shard_map/all_gather | solution.py:76
  159.2 14.1 %all_gather.19 = bf16[320,128]{0,1:T(8,128)(2,1)S(1)} all-gather(bf16[320,16]{0,1:T(8,128)(2,1)S(1)} %bitcast.228), channel_id=1, replica_groups=mesh['gx'=8,'gy'=4] {'gx'}, dimensions={1}, use_global_device_ids=true | all-gather | bytes 92160 | tf_op jit(solution)/shard_map/all_gather | solution.py:87
  175.1 1.8 fusion.3
  176.9 1.9 fusion
  180.5 2.3 collective-permute-start.12
  182.8 1.9 collective-permute-start.14
  187.4 3.9 %collective-permute-done.14 = f32[320,192]{0,1:T(8,128)S(1)} collective-permute-done((f32[320,192]{0,1:T(8,128)S(1)}, f32[320,192]{0,1:T(8,128)S(1)}, u32[]{:S(2)}, u32[]{:S(2)}) %collective-permute-start.14) | collective-permute-done | bytes 245792 | tf_op jit(solution)/shard_map/ppermute | solution.py:14
  191.3 8.2 %collective-permute-done.15 = f32[320,192]{0,1:T(8,128)S(1)} collective-permute-done((f32[320,192]{0,1:T(8,128)S(1)}, f32[320,192]{0,1:T(8,128)S(1)}, u32[]{:S(2)}, u32[]{:S(2)}) %collective-permute-start.15) | collective-permute-done | bytes 245792 | tf_op jit(solution)/shard_map/ppermute | solution.py:14
  201.8 2.0 collective-permute-start.16
  203.8 4.5 %collective-permute-start.18 = (f32[320,192]{0,1:T(8,128)}, f32[320,192]{0,1:T(8,128)}, u32[]{:S(2)}, u32[]{:S(2)}) collective-permute-start(f32[320,192]{0,1:T(8,128)} %get-tuple-element.25), channel_id=1, source_target_pairs={{0,1},{1,2},{2,3},{4,5},{5,6},{6,7},{8,9},{9,10},{10,11},{12,13},{... | collective-permute-start | bytes 737288 | tf_op jit(solution)/shard_map/ppermute | solution.py:14
  210.8 2.6 copy.29
  213.5 1.7 collective-permute-done.18
  215.2 6.6 %collective-permute-done.19 = f32[320,192]{0,1:T(8,128)} collective-permute-done((f32[320,192]{0,1:T(8,128)}, f32[320,192]{0,1:T(8,128)}, u32[]{:S(2)}, u32[]{:S(2)}) %collective-permute-start.19) | collective-permute-done | bytes 245792 | tf_op jit(solution)/shard_map/ppermute | solution.py:14
  224.9 38.5 %all-reduce.1 = (f32[320]{0:T(512)S(1)}, f32[320]{0:T(512)S(1)}) all-reduce(f32[320]{0:T(512)S(1)} %get-tuple-element.6, f32[320]{0:T(512)S(1)} %get-tuple-element.5), channel_id=1, replica_groups=mesh['gx'=8,'gy'=4] {'gx','gy'}, use_global_device_ids=true, to_apply=%region_5.6 | all-reduce | flops 640 | bytes 5120 | tf_op jit(solution)/shard_map/psum | solution.py:106
  263.5 2.4 multiply_add_fusion
  (159 shorter events, 41.4 us)
Async XLA Ops:
  0.0 83.7 %copy-start = (bf16[1,1,768,768]{3,2,1,0:T(8,128)(2,1)S(1)}, bf16[1,1,768,768]{3,2,1,0:T(8,128)(2,1)}, u32[]{:S(2)}) copy-start(bf16[1,1,768,768]{3,2,1,0:T(8,128)(2,1)} %param.8) | copy-start | bytes 3538948
  2.6 24.4 %collective-permute-start = (f32[320,192]{0,1:T(8,128)}, f32[320,192]{0,1:T(8,128)S(1)}, u32[]{:S(2)}, u32[]{:S(2)}) collective-permute-start(f32[320,192]{0,1:T(8,128)} %get-tuple-element.57), channel_id=1, source_target_pairs={{0,4},{4,8},{8,12},{12,16},{16,20},{20,24},{24,28},{1,5},{5,9},{9,... | collective-permute-start | bytes 737288 | tf_op jit(solution)/shard_map/ppermute | solution.py:14
  5.0 22.0 %collective-permute-start.2 = (f32[320,192]{0,1:T(8,128)}, f32[320,192]{0,1:T(8,128)S(1)}, u32[]{:S(2)}, u32[]{:S(2)}) collective-permute-start(f32[320,192]{0,1:T(8,128)} %get-tuple-element.58), channel_id=1, source_target_pairs={{0,1},{1,2},{2,3},{4,5},{5,6},{6,7},{8,9},{9,10},{10,11},{12,13},{... | collective-permute-start | bytes 737288 | tf_op jit(solution)/shard_map/ppermute | solution.py:14
  9.3 17.8 %collective-permute-start.3 = (f32[320,192]{0,1:T(8,128)}, f32[320,192]{0,1:T(8,128)S(1)}, u32[]{:S(2)}, u32[]{:S(2)}) collective-permute-start(f32[320,192]{0,1:T(8,128)} %get-tuple-element.59), channel_id=1, source_target_pairs={{1,0},{2,1},{3,2},{5,4},{6,5},{7,6},{9,8},{10,9},{11,10},{13,12},{... | collective-permute-start | bytes 737288 | tf_op jit(solution)/shard_map/ppermute | solution.py:14
  10.6 16.5 %collective-permute-start.1 = (f32[320,192]{0,1:T(8,128)S(1)}, f32[320,192]{0,1:T(8,128)}, u32[]{:S(2)}, u32[]{:S(2)}) collective-permute-start(f32[320,192]{0,1:T(8,128)S(1)} %get-tuple-element.60), channel_id=1, source_target_pairs={{4,0},{8,4},{12,8},{16,12},{20,16},{24,20},{28,24},{5,1},{9,5},{13... | collective-permute-start | bytes 737288 | tf_op jit(solution)/shard_map/ppermute | solution.py:14
  29.4 28.2 %copy-start.32 = (f32[1,32,32]{2,1,0:T(8,128)S(1)}, f32[1,32,32]{2,1,0:T(8,128)}, u32[]{:S(2)}) copy-start(f32[1,32,32]{2,1,0:T(8,128)} %param.11) | copy-start | bytes 12292
  29.4 29.4 %copy-start.1 = (bf16[1,1,768,768]{3,2,1,0:T(8,128)(2,1)S(1)}, bf16[1,1,768,768]{3,2,1,0:T(8,128)(2,1)}, u32[]{:S(2)}) copy-start(bf16[1,1,768,768]{3,2,1,0:T(8,128)(2,1)} %param.9) | copy-start | bytes 3538948
  64.3 6.8 %collective-permute-start.4 = (f32[320,192]{0,1:T(8,128)S(1)}, f32[320,192]{0,1:T(8,128)S(1)}, u32[]{:S(2)}, u32[]{:S(2)}) collective-permute-start(f32[320,192]{0,1:T(8,128)S(1)} %get-tuple-element.49), channel_id=1, source_target_pairs={{0,4},{4,8},{8,12},{12,16},{16,20},{20,24},{24,28},{1,5},{5,9},{9,... | collective-permute-start | bytes 737288 | tf_op jit(solution)/shard_map/ppermute | solution.py:14
  66.6 8.6 %collective-permute-start.6 = (f32[320,192]{0,1:T(8,128)S(1)}, f32[320,192]{0,1:T(8,128)S(1)}, u32[]{:S(2)}, u32[]{:S(2)}) collective-permute-start(f32[320,192]{0,1:T(8,128)S(1)} %get-tuple-element.50), channel_id=1, source_target_pairs={{0,1},{1,2},{2,3},{4,5},{5,6},{6,7},{8,9},{9,10},{10,11},{12,13},{... | collective-permute-start | bytes 737288 | tf_op jit(solution)/shard_map/ppermute | solution.py:14
  68.5 14.9 %collective-permute-start.7 = (f32[320,192]{0,1:T(8,128)S(1)}, f32[320,192]{0,1:T(8,128)S(1)}, u32[]{:S(2)}, u32[]{:S(2)}) collective-permute-start(f32[320,192]{0,1:T(8,128)S(1)} %get-tuple-element.51), channel_id=1, source_target_pairs={{1,0},{2,1},{3,2},{5,4},{6,5},{7,6},{9,8},{10,9},{11,10},{13,12},{... | collective-permute-start | bytes 737288 | tf_op jit(solution)/shard_map/ppermute | solution.py:14
  69.8 13.6 %collective-permute-start.5 = (f32[320,192]{0,1:T(8,128)S(1)}, f32[320,192]{0,1:T(8,128)S(1)}, u32[]{:S(2)}, u32[]{:S(2)}) collective-permute-start(f32[320,192]{0,1:T(8,128)S(1)} %get-tuple-element.52), channel_id=1, source_target_pairs={{4,0},{8,4},{12,8},{16,12},{20,16},{24,20},{28,24},{5,1},{9,5},{13... | collective-permute-start | bytes 737288 | tf_op jit(solution)/shard_map/ppermute | solution.py:14
  84.6 7.9 %collective-permute-start.8 = (f32[320,192]{0,1:T(8,128)S(1)}, f32[320,192]{0,1:T(8,128)S(1)}, u32[]{:S(2)}, u32[]{:S(2)}) collective-permute-start(f32[320,192]{0,1:T(8,128)S(1)} %get-tuple-element.41), channel_id=1, source_target_pairs={{0,4},{4,8},{8,12},{12,16},{16,20},{20,24},{24,28},{1,5},{5,9},{9,... | collective-permute-start | bytes 737288 | tf_op jit(solution)/shard_map/ppermute | solution.py:14
  86.0 11.0 %collective-permute-start.10 = (f32[320,192]{0,1:T(8,128)S(1)}, f32[320,192]{0,1:T(8,128)S(1)}, u32[]{:S(2)}, u32[]{:S(2)}) collective-permute-start(f32[320,192]{0,1:T(8,128)S(1)} %get-tuple-element.42), channel_id=1, source_target_pairs={{0,1},{1,2},{2,3},{4,5},{5,6},{6,7},{8,9},{9,10},{10,11},{12,13},{... | collective-permute-start | bytes 737288 | tf_op jit(solution)/shard_map/ppermute | solution.py:14
  89.9 13.6 %collective-permute-start.11 = (f32[320,192]{0,1:T(8,128)S(1)}, f32[320,192]{0,1:T(8,128)S(1)}, u32[]{:S(2)}, u32[]{:S(2)}) collective-permute-start(f32[320,192]{0,1:T(8,128)S(1)} %get-tuple-element.43), channel_id=1, source_target_pairs={{1,0},{2,1},{3,2},{5,4},{6,5},{7,6},{9,8},{10,9},{11,10},{13,12},{... | collective-permute-start | bytes 737288 | tf_op jit(solution)/shard_map/ppermute | solution.py:14
  91.3 12.2 %collective-permute-start.9 = (f32[320,192]{0,1:T(8,128)S(1)}, f32[320,192]{0,1:T(8,128)S(1)}, u32[]{:S(2)}, u32[]{:S(2)}) collective-permute-start(f32[320,192]{0,1:T(8,128)S(1)} %get-tuple-element.44), channel_id=1, source_target_pairs={{4,0},{8,4},{12,8},{16,12},{20,16},{24,20},{28,24},{5,1},{9,5},{13... | collective-permute-start | bytes 737288 | tf_op jit(solution)/shard_map/ppermute | solution.py:14
  103.7 42.0 %copy-start.13 = (f32[320,1,192]{0,2,1:T(8,128)S(1)}, f32[320,1,192]{0,2,1:T(8,128)}, u32[]{:S(2)}) copy-start(f32[320,1,192]{0,2,1:T(8,128)} %copy-done.12) | copy-start | bytes 737284
  103.7 42.0 %copy-start.15 = (f32[320,1,192]{0,2,1:T(8,128)S(1)}, f32[320,1,192]{0,2,1:T(8,128)}, u32[]{:S(2)}) copy-start(f32[320,1,192]{0,2,1:T(8,128)} %copy-done.14) | copy-start | bytes 737284
  103.7 42.0 %copy-start.17 = (f32[320,1,192]{0,2,1:T(8,128)S(1)}, f32[320,1,192]{0,2,1:T(8,128)}, u32[]{:S(2)}) copy-start(f32[320,1,192]{0,2,1:T(8,128)} %copy-done.16) | copy-start | bytes 737284
  103.7 42.0 %copy-start.19 = (f32[320,1,192]{0,2,1:T(8,128)S(1)}, f32[320,1,192]{0,2,1:T(8,128)}, u32[]{:S(2)}) copy-start(f32[320,1,192]{0,2,1:T(8,128)} %copy-done.18) | copy-start | bytes 737284
  148.1 27.0 %copy-start.2 = (bf16[1,1,768,768]{3,2,1,0:T(8,128)(2,1)S(1)}, bf16[1,1,768,768]{3,2,1,0:T(8,128)(2,1)}, u32[]{:S(2)}) copy-start(bf16[1,1,768,768]{3,2,1,0:T(8,128)(2,1)} %param.9) | copy-start | bytes 3538948
  180.5 6.8 %collective-permute-start.12 = (f32[320,192]{0,1:T(8,128)S(1)}, f32[320,192]{0,1:T(8,128)S(1)}, u32[]{:S(2)}, u32[]{:S(2)}) collective-permute-start(f32[320,192]{0,1:T(8,128)S(1)} %get-tuple-element.33), channel_id=1, source_target_pairs={{0,4},{4,8},{8,12},{12,16},{16,20},{20,24},{24,28},{1,5},{5,9},{9,... | collective-permute-start | bytes 737288 | tf_op jit(solution)/shard_map/ppermute | solution.py:14
  182.8 8.5 %collective-permute-start.14 = (f32[320,192]{0,1:T(8,128)S(1)}, f32[320,192]{0,1:T(8,128)S(1)}, u32[]{:S(2)}, u32[]{:S(2)}) collective-permute-start(f32[320,192]{0,1:T(8,128)S(1)} %get-tuple-element.34), channel_id=1, source_target_pairs={{0,1},{1,2},{2,3},{4,5},{5,6},{6,7},{8,9},{9,10},{10,11},{12,13},{... | collective-permute-start | bytes 737288 | tf_op jit(solution)/shard_map/ppermute | solution.py:14
  184.8 14.8 %collective-permute-start.15 = (f32[320,192]{0,1:T(8,128)S(1)}, f32[320,192]{0,1:T(8,128)S(1)}, u32[]{:S(2)}, u32[]{:S(2)}) collective-permute-start(f32[320,192]{0,1:T(8,128)S(1)} %get-tuple-element.35), channel_id=1, source_target_pairs={{1,0},{2,1},{3,2},{5,4},{6,5},{7,6},{9,8},{10,9},{11,10},{13,12},{... | collective-permute-start | bytes 737288 | tf_op jit(solution)/shard_map/ppermute | solution.py:14
  186.1 13.5 %collective-permute-start.13 = (f32[320,192]{0,1:T(8,128)S(1)}, f32[320,192]{0,1:T(8,128)S(1)}, u32[]{:S(2)}, u32[]{:S(2)}) collective-permute-start(f32[320,192]{0,1:T(8,128)S(1)} %get-tuple-element.36), channel_id=1, source_target_pairs={{4,0},{8,4},{12,8},{16,12},{20,16},{24,20},{28,24},{5,1},{9,5},{13... | collective-permute-start | bytes 737288 | tf_op jit(solution)/shard_map/ppermute | solution.py:14
  201.8 11.7 %collective-permute-start.16 = (f32[320,192]{0,1:T(8,128)}, f32[320,192]{0,1:T(8,128)}, u32[]{:S(2)}, u32[]{:S(2)}) collective-permute-start(f32[320,192]{0,1:T(8,128)} %get-tuple-element.24), channel_id=1, source_target_pairs={{0,4},{4,8},{8,12},{12,16},{16,20},{20,24},{24,28},{1,5},{5,9},{9,... | collective-permute-start | bytes 737288 | tf_op jit(solution)/shard_map/ppermute | solution.py:14
  203.8 11.4 %collective-permute-start.18 = (f32[320,192]{0,1:T(8,128)}, f32[320,192]{0,1:T(8,128)}, u32[]{:S(2)}, u32[]{:S(2)}) collective-permute-start(f32[320,192]{0,1:T(8,128)} %get-tuple-element.25), channel_id=1, source_target_pairs={{0,1},{1,2},{2,3},{4,5},{5,6},{6,7},{8,9},{9,10},{10,11},{12,13},{... | collective-permute-start | bytes 737288 | tf_op jit(solution)/shard_map/ppermute | solution.py:14
  208.3 13.5 %collective-permute-start.19 = (f32[320,192]{0,1:T(8,128)}, f32[320,192]{0,1:T(8,128)}, u32[]{:S(2)}, u32[]{:S(2)}) collective-permute-start(f32[320,192]{0,1:T(8,128)} %get-tuple-element.26), channel_id=1, source_target_pairs={{1,0},{2,1},{3,2},{5,4},{6,5},{7,6},{9,8},{10,9},{11,10},{13,12},{... | collective-permute-start | bytes 737288 | tf_op jit(solution)/shard_map/ppermute | solution.py:14
  209.5 12.2 %collective-permute-start.17 = (f32[320,192]{0,1:T(8,128)}, f32[320,192]{0,1:T(8,128)}, u32[]{:S(2)}, u32[]{:S(2)}) collective-permute-start(f32[320,192]{0,1:T(8,128)} %get-tuple-element.27), channel_id=1, source_target_pairs={{4,0},{8,4},{12,8},{16,12},{20,16},{24,20},{28,24},{5,1},{9,5},{13... | collective-permute-start | bytes 737288 | tf_op jit(solution)/shard_map/ppermute | solution.py:14
  223.6 39.9 %copy-start.41 = (f32[320]{0:T(512)S(1)}, f32[320]{0:T(512)}, u32[]{:S(2)}) copy-start(f32[320]{0:T(512)} %copy-done.40) | copy-start | bytes 3844
  223.6 39.8 %copy-start.43 = (f32[320]{0:T(512)S(1)}, f32[320]{0:T(512)}, u32[]{:S(2)}) copy-start(f32[320]{0:T(512)} %copy-done.42) | copy-start | bytes 3844
  223.6 39.9 %copy-start.3 = (f32[1,1,320,768]{3,2,1,0:T(8,128)S(1)}, f32[1,1,320,768]{3,2,1,0:T(8,128)}, u32[]{:S(2)}) copy-start(f32[1,1,320,768]{3,2,1,0:T(8,128)} %copy.29) | copy-start | bytes 2949124
  223.6 39.9 %copy-start.36 = (f32[320]{0:T(512)S(1)}, f32[320]{0:T(512)}, u32[]{:S(2)}) copy-start(f32[320]{0:T(512)} %copy-done.35) | copy-start | bytes 3844
  (35 other events, 132.7 us)
where the time goes:
time: 267 us; the launch traced here: 266 us
  blocking collectives  137 us (51%)
  waiting for transfers between devices  43.7 us (16%)
  starting transfers between devices  39.7 us (15%)
  local copies, waits for them, and re-layouts  16.6 us (6%)
  matrix products  15.7 us (6%)
  other arithmetic  11.6 us (4%)
    psum x2, blocking collectives, paired(): return lax.psum((inner(resid, zvec), inner(zvec, wvec)), ('gx', 'gy'))  77.9 us
    ppermute x20, waiting for transfers between devices, from_behind(): lax.ppermute(value, axis, [(source, source + steps) for source in range(f...  43.7 us
    ppermute x20, starting transfers between devices, from_behind(): lax.ppermute(value, axis, [(source, source + steps) for source in range(f...  39.7 us
    all_gather x2, blocking collectives, precondition(): everyone = lax.all_gather(summed, 'gx', axis=1, tiled=True)  28.5 us
    all_gather x2, blocking collectives, precondition(): grouped = lax.all_gather(primal, 'gy', axis=1, tiled=True)  18.1 us
    unnamed x1, blocking collectives  12.4 us
    dot_general x6, matrix products, contract_last(): lax.dot_general(left, right, (((1,), (1,)), ((), ())), preferred_element_...  6.75 us
  transfers between devices with their start and end apart: 20, of which 8 were waited for; matrix products, arithmetic and copies ran while one was open for 2% of the time, Pallas kernels for 0%

commit v1 on v0

--- a/solution.py
+++ b/solution.py
@@ -103,7 +103,7 @@
     resid = rhs
 
     def paired(resid, zvec, wvec):
-        return lax.psum((inner(resid, zvec), inner(zvec, wvec)), ("gx", "gy"))
+        return lax.psum(lax.psum((inner(resid, zvec), inner(zvec, wvec)), "gy"), "gx")
 
     zvec = precondition(resid)
     wvec = apply(zvec)

time: 267 us -> 230 us (0.86)
  blocking collectives: 137 us -> 101 us
    psum x2 -> x4, blocking collectives: 77.9 us -> 42.2 us  [the longest x2 27.2 us: paired(): lax.psum(lax.psum((inner(resid, zvec), inner(zvec, wvec)), 'gy'), 'gx')]
  transfers between devices with their start and end apart: 20 -> 20, of which waited for: 8 -> 7; matrix products, arithmetic and copies ran while one was open for 2% -> 2% of each run, Pallas kernels for 0% -> 0%
where the time goes in v1:
time: 230 us; the launch traced here: 228 us
  blocking collectives  101 us (44%)
  waiting for transfers between devices  42.3 us (18%)
  starting transfers between devices  39.8 us (17%)
  local copies, waits for them, and re-layouts  16.7 us (7%)
  matrix products  15.7 us (7%)
  other arithmetic  11.6 us (5%)
    ppermute x20, waiting for transfers between devices, from_behind(): lax.ppermute(value, axis, [(source, source + steps) for source in range(f...  42.3 us
    ppermute x20, starting transfers between devices, from_behind(): lax.ppermute(value, axis, [(source, source + steps) for source in range(f...  39.8 us
    all_gather x2, blocking collectives, precondition(): everyone = lax.all_gather(summed, 'gx', axis=1, tiled=True)  28.5 us
    psum x2, blocking collectives, paired(): lax.psum(lax.psum((inner(resid, zvec), inner(zvec, wvec)), 'gy'), 'gx')  27.2 us
    all_gather x2, blocking collectives, precondition(): grouped = lax.all_gather(primal, 'gy', axis=1, tiled=True)  17.8 us
    psum x2, blocking collectives, paired(): lax.psum((inner(resid, zvec), inner(zvec, wvec)), 'gy')  15 us
    unnamed x1, blocking collectives  12.3 us
    dot_general x6, matrix products, contract_last(): lax.dot_general(left, right, (((1,), (1,)), ((), ())), preferred_element_...  6.74 us
  transfers between devices with their start and end apart: 20, of which 7 were waited for; matrix products, arithmetic and copies ran while one was open for 2% of the time, Pallas kernels for 0%

profile of v1, /device:TPU:0, one launch (start us, length us, event | category | flops | bytes accessed | tf_op | source)
XLA Modules:
  0.0 228.5 jit_solution(17186882076321234395)
XLA Ops:
  2.6 2.4 %collective-permute-start = (f32[320,192]{0,1:T(8,128)}, f32[320,192]{0,1:T(8,128)S(1)}, u32[]{:S(2)}, u32[]{:S(2)}) collective-permute-start(f32[320,192]{0,1:T(8,128)} %get-tuple-element.61), channel_id=1, source_target_pairs={{0,4},{4,8},{8,12},{12,16},{16,20},{20,24},{24,28},{1,5},{5,9},{9,... | collective-permute-start | bytes 737288 | tf_op jit(solution)/shard_map/ppermute | solution.py:14
  5.0 4.2 %collective-permute-start.2 = (f32[320,192]{0,1:T(8,128)}, f32[320,192]{0,1:T(8,128)S(1)}, u32[]{:S(2)}, u32[]{:S(2)}) collective-permute-start(f32[320,192]{0,1:T(8,128)} %get-tuple-element.62), channel_id=1, source_target_pairs={{0,1},{1,2},{2,3},{4,5},{5,6},{6,7},{8,9},{9,10},{10,11},{12,13},{... | collective-permute-start | bytes 737288 | tf_op jit(solution)/shard_map/ppermute | solution.py:14
  13.9 12.3 %all-reduce = s32[4]{0:T(128)} all-reduce(s32[4]{0:T(128)S(1)} %bitcast_dynamic-update-slice_fusion), channel_id=2, replica_groups=mesh['gx'=8,'gy'=4] {'gy'}, use_global_device_ids=true, to_apply=%add | all-reduce | flops 4 | bytes 32
  30.1 9.1 %all_gather.15 = f32[320,32]{0,1:T(8,128)S(1)} all-gather(f32[320,8]{0,1:T(8,128)S(1)} %fusion.18), channel_id=1, replica_groups=mesh['gx'=8,'gy'=4] {'gy'}, dimensions={1}, use_global_device_ids=true | all-gather | bytes 51200 | tf_op jit(solution)/shard_map/all_gather | solution.py:76
  40.1 14.4 %all_gather.17 = bf16[320,128]{0,1:T(8,128)(2,1)S(1)} all-gather(bf16[320,16]{0,1:T(8,128)(2,1)S(1)} %bitcast.227), channel_id=1, replica_groups=mesh['gx'=8,'gy'=4] {'gx'}, dimensions={1}, use_global_device_ids=true | all-gather | bytes 92160 | tf_op jit(solution)/shard_map/all_gather | solution.py:87
  58.9 1.8 fusion.5
  60.7 1.9 fusion.1
  64.3 2.3 collective-permute-start.4
  66.6 1.9 collective-permute-start.6
  71.1 4.2 %collective-permute-done.6 = f32[320,192]{0,1:T(8,128)S(1)} collective-permute-done((f32[320,192]{0,1:T(8,128)S(1)}, f32[320,192]{0,1:T(8,128)S(1)}, u32[]{:S(2)}, u32[]{:S(2)}) %collective-permute-start.6) | collective-permute-done | bytes 245792 | tf_op jit(solution)/shard_map/ppermute | solution.py:14
  75.3 8.2 %collective-permute-done.7 = f32[320,192]{0,1:T(8,128)S(1)} collective-permute-done((f32[320,192]{0,1:T(8,128)S(1)}, f32[320,192]{0,1:T(8,128)S(1)}, u32[]{:S(2)}, u32[]{:S(2)}) %collective-permute-start.7) | collective-permute-done | bytes 245792 | tf_op jit(solution)/shard_map/ppermute | solution.py:14
  86.2 3.8 %collective-permute-start.10 = (f32[320,192]{0,1:T(8,128)S(1)}, f32[320,192]{0,1:T(8,128)S(1)}, u32[]{:S(2)}, u32[]{:S(2)}) collective-permute-start(f32[320,192]{0,1:T(8,128)S(1)} %get-tuple-element.46), channel_id=1, source_target_pairs={{0,1},{1,2},{2,3},{4,5},{5,6},{6,7},{8,9},{9,10},{10,11},{12,13},{... | collective-permute-start | bytes 737288 | tf_op jit(solution)/shard_map/ppermute | solution.py:14
  92.6 4.4 %collective-permute-done.10 = f32[320,192]{0,1:T(8,128)S(1)} collective-permute-done((f32[320,192]{0,1:T(8,128)S(1)}, f32[320,192]{0,1:T(8,128)S(1)}, u32[]{:S(2)}, u32[]{:S(2)}) %collective-permute-start.10) | collective-permute-done | bytes 245792 | tf_op jit(solution)/shard_map/ppermute | solution.py:14
  97.0 6.5 %collective-permute-done.11 = f32[320,192]{0,1:T(8,128)S(1)} collective-permute-done((f32[320,192]{0,1:T(8,128)S(1)}, f32[320,192]{0,1:T(8,128)S(1)}, u32[]{:S(2)}, u32[]{:S(2)}) %collective-permute-start.11) | collective-permute-done | bytes 245792 | tf_op jit(solution)/shard_map/ppermute | solution.py:14
  103.7 2.0 multiply_reduce_fusion.1
  105.7 7.6 %all-reduce.4 = (f32[320]{0:T(512)S(1)}, f32[320]{0:T(512)S(1)}) all-reduce(f32[320]{0:T(512)} %get-tuple-element.8, f32[320]{0:T(512)} %get-tuple-element.7), channel_id=1, replica_groups=mesh['gx'=8,'gy'=4] {'gy'}, use_global_device_ids=true, to_apply=%region_1.2 | all-reduce | flops 640 | bytes 5120 | tf_op jit(solution)/shard_map/psum | solution.py:106
  113.3 13.6 %all-reduce.2 = (f32[320]{0:T(512)S(1)}, f32[320]{0:T(512)S(1)}) all-reduce(f32[320]{0:T(512)S(1)} %get-tuple-element.15, f32[320]{0:T(512)S(1)} %get-tuple-element.16), channel_id=1, replica_groups=mesh['gx'=8,'gy'=4] {'gx'}, use_global_device_ids=true, to_apply=%region_2.3 | all-reduce | flops 640 | bytes 5120 | tf_op jit(solution)/shard_map/psum | solution.py:106
  127.6 2.4 %fusion.42 = (bf16[320,4,192]{0,2,1:T(8,128)(2,1)}, f32[320,4,192]{0,2,1:T(8,128)S(1)}) fusion(f32[320,1,192]{0,2,1:T(8,128)} %copy-done.21, f32[320,1,192]{0,2,1:T(8,128)} %copy-done.22, f32[320,1,192]{0,2,1:T(8,128)} %copy-done.23, f32[320,1,192]{0,2,1:T(8,128)} %copy-done.20, f32[320]{0:T(512)S(1)} %div.12, f32[320,1,192]{0,2,1:T(8,128)S(1)} %copy-done.15, ...), kind=kLoop, calls=%fused_computation.107 | loop fusion | flops 2457600 | bytes 3441936 | tf_op jit(solution)/shard_map/convert_element_type | solution.py:74
  130.7 8.7 %all_gather.18 = f32[320,32]{0,1:T(8,128)S(1)} all-gather(f32[320,8]{0,1:T(8,128)S(1)} %fusion.15), channel_id=1, replica_groups=mesh['gx'=8,'gy'=4] {'gy'}, dimensions={1}, use_global_device_ids=true | all-gather | bytes 51200 | tf_op jit(solution)/shard_map/all_gather | solution.py:76
  140.7 14.1 %all_gather.19 = bf16[320,128]{0,1:T(8,128)(2,1)S(1)} all-gather(bf16[320,16]{0,1:T(8,128)(2,1)S(1)} %bitcast.228), channel_id=1, replica_groups=mesh['gx'=8,'gy'=4] {'gx'}, dimensions={1}, use_global_device_ids=true | all-gather | bytes 92160 | tf_op jit(solution)/shard_map/all_gather | solution.py:87
  158.5 1.9 fusion
  162.0 2.3 collective-permute-start.12
  164.3 2.5 %collective-permute-start.14 = (f32[320,192]{0,1:T(8,128)S(1)}, f32[320,192]{0,1:T(8,128)S(1)}, u32[]{:S(2)}, u32[]{:S(2)}) collective-permute-start(f32[320,192]{0,1:T(8,128)S(1)} %get-tuple-element.38), channel_id=1, source_target_pairs={{0,1},{1,2},{2,3},{4,5},{5,6},{6,7},{8,9},{9,10},{10,11},{12,13},{... | collective-permute-start | bytes 737288 | tf_op jit(solution)/shard_map/ppermute | solution.py:14
  169.5 3.8 %collective-permute-done.14 = f32[320,192]{0,1:T(8,128)S(1)} collective-permute-done((f32[320,192]{0,1:T(8,128)S(1)}, f32[320,192]{0,1:T(8,128)S(1)}, u32[]{:S(2)}, u32[]{:S(2)}) %collective-permute-start.14) | collective-permute-done | bytes 245792 | tf_op jit(solution)/shard_map/ppermute | solution.py:14
  173.3 8.2 %collective-permute-done.15 = f32[320,192]{0,1:T(8,128)S(1)} collective-permute-done((f32[320,192]{0,1:T(8,128)S(1)}, f32[320,192]{0,1:T(8,128)S(1)}, u32[]{:S(2)}, u32[]{:S(2)}) %collective-permute-start.15) | collective-permute-done | bytes 245792 | tf_op jit(solution)/shard_map/ppermute | solution.py:14
  183.7 2.0 collective-permute-start.16
  185.7 4.0 %collective-permute-start.18 = (f32[320,192]{0,1:T(8,128)}, f32[320,192]{0,1:T(8,128)}, u32[]{:S(2)}, u32[]{:S(2)}) collective-permute-start(f32[320,192]{0,1:T(8,128)} %get-tuple-element.29), channel_id=1, source_target_pairs={{0,1},{1,2},{2,3},{4,5},{5,6},{6,7},{8,9},{9,10},{10,11},{12,13},{... | collective-permute-start | bytes 737288 | tf_op jit(solution)/shard_map/ppermute | solution.py:14
  192.4 2.6 %copy.29 = f32[1,1,320,768]{3,2,1,0:T(8,128)} copy(f32[1,1,320,768]{2,3,1,0:T(8,128)} %bitcast.219) | data formatting | bytes 1966080 | tf_op jit(solution)/shard_map/reshape | solution.py:26
  195.0 6.9 %collective-permute-done.19 = f32[320,192]{0,1:T(8,128)} collective-permute-done((f32[320,192]{0,1:T(8,128)}, f32[320,192]{0,1:T(8,128)}, u32[]{:S(2)}, u32[]{:S(2)}) %collective-permute-start.19) | collective-permute-done | bytes 245792 | tf_op jit(solution)/shard_map/ppermute | solution.py:14
  205.0 7.4 %all-reduce.3 = (f32[320]{0:T(512)S(1)}, f32[320]{0:T(512)S(1)}) all-reduce(f32[320]{0:T(512)S(1)} %get-tuple-element.6, f32[320]{0:T(512)S(1)} %get-tuple-element.5), channel_id=1, replica_groups=mesh['gx'=8,'gy'=4] {'gy'}, use_global_device_ids=true, to_apply=%region_7.8 | all-reduce | flops 640 | bytes 5120 | tf_op jit(solution)/shard_map/psum | solution.py:106
  212.5 13.6 %all-reduce.1 = (f32[320]{0:T(512)S(1)}, f32[320]{0:T(512)S(1)}) all-reduce(f32[320]{0:T(512)S(1)} %get-tuple-element.13, f32[320]{0:T(512)S(1)} %get-tuple-element.14), channel_id=1, replica_groups=mesh['gx'=8,'gy'=4] {'gx'}, use_global_device_ids=true, to_apply=%region_8.9 | all-reduce | flops 640 | bytes 5120 | tf_op jit(solution)/shard_map/psum | solution.py:106
  226.1 2.4 %multiply_add_fusion = f32[1,1,320,768]{3,2,1,0:T(8,128)} fusion(f32[1,1,320,768]{3,2,1,0:T(8,128)} %copy.35, f32[1,1,320,768]{3,2,1,0:T(8,128)S(1)} %copy-done.3, f32[320]{0:T(512)S(1)} %get-tuple-element.18, f32[320]{0:T(512)S(1)} %get-tuple-element.17, f32[320]{0:T(512)S(1)} %copy-done.36), kind=kLoop, calls=%fused_computation.24 | loop fusion | flops 1228800 | bytes 2952960 | tf_op jit(solution)/shard_map/add | solution.py:114
  (161 shorter events, 43.4 us)
Async XLA Ops:
  0.0 83.9 %copy-start = (bf16[1,1,768,768]{3,2,1,0:T(8,128)(2,1)S(1)}, bf16[1,1,768,768]{3,2,1,0:T(8,128)(2,1)}, u32[]{:S(2)}) copy-start(bf16[1,1,768,768]{3,2,1,0:T(8,128)(2,1)} %param.8) | copy-start | bytes 3538948
  2.6 24.4 %collective-permute-start = (f32[320,192]{0,1:T(8,128)}, f32[320,192]{0,1:T(8,128)S(1)}, u32[]{:S(2)}, u32[]{:S(2)}) collective-permute-start(f32[320,192]{0,1:T(8,128)} %get-tuple-element.61), channel_id=1, source_target_pairs={{0,4},{4,8},{8,12},{12,16},{16,20},{20,24},{24,28},{1,5},{5,9},{9,... | collective-permute-start | bytes 737288 | tf_op jit(solution)/shard_map/ppermute | solution.py:14
  5.0 22.0 %collective-permute-start.2 = (f32[320,192]{0,1:T(8,128)}, f32[320,192]{0,1:T(8,128)S(1)}, u32[]{:S(2)}, u32[]{:S(2)}) collective-permute-start(f32[320,192]{0,1:T(8,128)} %get-tuple-element.62), channel_id=1, source_target_pairs={{0,1},{1,2},{2,3},{4,5},{5,6},{6,7},{8,9},{9,10},{10,11},{12,13},{... | collective-permute-start | bytes 737288 | tf_op jit(solution)/shard_map/ppermute | solution.py:14
  9.3 17.8 %collective-permute-start.3 = (f32[320,192]{0,1:T(8,128)}, f32[320,192]{0,1:T(8,128)S(1)}, u32[]{:S(2)}, u32[]{:S(2)}) collective-permute-start(f32[320,192]{0,1:T(8,128)} %get-tuple-element.63), channel_id=1, source_target_pairs={{1,0},{2,1},{3,2},{5,4},{6,5},{7,6},{9,8},{10,9},{11,10},{13,12},{... | collective-permute-start | bytes 737288 | tf_op jit(solution)/shard_map/ppermute | solution.py:14
  10.6 16.5 %collective-permute-start.1 = (f32[320,192]{0,1:T(8,128)S(1)}, f32[320,192]{0,1:T(8,128)}, u32[]{:S(2)}, u32[]{:S(2)}) collective-permute-start(f32[320,192]{0,1:T(8,128)S(1)} %get-tuple-element.64), channel_id=1, source_target_pairs={{4,0},{8,4},{12,8},{16,12},{20,16},{24,20},{28,24},{5,1},{9,5},{13... | collective-permute-start | bytes 737288 | tf_op jit(solution)/shard_map/ppermute | solution.py:14
  29.4 28.2 %copy-start.32 = (f32[1,32,32]{2,1,0:T(8,128)S(1)}, f32[1,32,32]{2,1,0:T(8,128)}, u32[]{:S(2)}) copy-start(f32[1,32,32]{2,1,0:T(8,128)} %param.11) | copy-start | bytes 12292
  29.4 29.4 %copy-start.1 = (bf16[1,1,768,768]{3,2,1,0:T(8,128)(2,1)S(1)}, bf16[1,1,768,768]{3,2,1,0:T(8,128)(2,1)}, u32[]{:S(2)}) copy-start(bf16[1,1,768,768]{3,2,1,0:T(8,128)(2,1)} %param.9) | copy-start | bytes 3538948
  64.3 6.8 %collective-permute-start.4 = (f32[320,192]{0,1:T(8,128)S(1)}, f32[320,192]{0,1:T(8,128)S(1)}, u32[]{:S(2)}, u32[]{:S(2)}) collective-permute-start(f32[320,192]{0,1:T(8,128)S(1)} %get-tuple-element.53), channel_id=1, source_target_pairs={{0,4},{4,8},{8,12},{12,16},{16,20},{20,24},{24,28},{1,5},{5,9},{9,... | collective-permute-start | bytes 737288 | tf_op jit(solution)/shard_map/ppermute | solution.py:14
  66.6 8.7 %collective-permute-start.6 = (f32[320,192]{0,1:T(8,128)S(1)}, f32[320,192]{0,1:T(8,128)S(1)}, u32[]{:S(2)}, u32[]{:S(2)}) collective-permute-start(f32[320,192]{0,1:T(8,128)S(1)} %get-tuple-element.54), channel_id=1, source_target_pairs={{0,1},{1,2},{2,3},{4,5},{5,6},{6,7},{8,9},{9,10},{10,11},{12,13},{... | collective-permute-start | bytes 737288 | tf_op jit(solution)/shard_map/ppermute | solution.py:14
  68.5 15.0 %collective-permute-start.7 = (f32[320,192]{0,1:T(8,128)S(1)}, f32[320,192]{0,1:T(8,128)S(1)}, u32[]{:S(2)}, u32[]{:S(2)}) collective-permute-start(f32[320,192]{0,1:T(8,128)S(1)} %get-tuple-element.55), channel_id=1, source_target_pairs={{1,0},{2,1},{3,2},{5,4},{6,5},{7,6},{9,8},{10,9},{11,10},{13,12},{... | collective-permute-start | bytes 737288 | tf_op jit(solution)/shard_map/ppermute | solution.py:14
  69.8 13.7 %collective-permute-start.5 = (f32[320,192]{0,1:T(8,128)S(1)}, f32[320,192]{0,1:T(8,128)S(1)}, u32[]{:S(2)}, u32[]{:S(2)}) collective-permute-start(f32[320,192]{0,1:T(8,128)S(1)} %get-tuple-element.56), channel_id=1, source_target_pairs={{4,0},{8,4},{12,8},{16,12},{20,16},{24,20},{28,24},{5,1},{9,5},{13... | collective-permute-start | bytes 737288 | tf_op jit(solution)/shard_map/ppermute | solution.py:14
  84.7 7.8 %collective-permute-start.8 = (f32[320,192]{0,1:T(8,128)S(1)}, f32[320,192]{0,1:T(8,128)S(1)}, u32[]{:S(2)}, u32[]{:S(2)}) collective-permute-start(f32[320,192]{0,1:T(8,128)S(1)} %get-tuple-element.45), channel_id=1, source_target_pairs={{0,4},{4,8},{8,12},{12,16},{16,20},{20,24},{24,28},{1,5},{5,9},{9,... | collective-permute-start | bytes 737288 | tf_op jit(solution)/shard_map/ppermute | solution.py:14
  86.2 10.8 %collective-permute-start.10 = (f32[320,192]{0,1:T(8,128)S(1)}, f32[320,192]{0,1:T(8,128)S(1)}, u32[]{:S(2)}, u32[]{:S(2)}) collective-permute-start(f32[320,192]{0,1:T(8,128)S(1)} %get-tuple-element.46), channel_id=1, source_target_pairs={{0,1},{1,2},{2,3},{4,5},{5,6},{6,7},{8,9},{9,10},{10,11},{12,13},{... | collective-permute-start | bytes 737288 | tf_op jit(solution)/shard_map/ppermute | solution.py:14
  90.0 13.5 %collective-permute-start.11 = (f32[320,192]{0,1:T(8,128)S(1)}, f32[320,192]{0,1:T(8,128)S(1)}, u32[]{:S(2)}, u32[]{:S(2)}) collective-permute-start(f32[320,192]{0,1:T(8,128)S(1)} %get-tuple-element.47), channel_id=1, source_target_pairs={{1,0},{2,1},{3,2},{5,4},{6,5},{7,6},{9,8},{10,9},{11,10},{13,12},{... | collective-permute-start | bytes 737288 | tf_op jit(solution)/shard_map/ppermute | solution.py:14
  91.3 12.2 %collective-permute-start.9 = (f32[320,192]{0,1:T(8,128)S(1)}, f32[320,192]{0,1:T(8,128)S(1)}, u32[]{:S(2)}, u32[]{:S(2)}) collective-permute-start(f32[320,192]{0,1:T(8,128)S(1)} %get-tuple-element.48), channel_id=1, source_target_pairs={{4,0},{8,4},{12,8},{16,12},{20,16},{24,20},{28,24},{5,1},{9,5},{13... | collective-permute-start | bytes 737288 | tf_op jit(solution)/shard_map/ppermute | solution.py:14
  103.7 23.8 %copy-start.13 = (f32[320,1,192]{0,2,1:T(8,128)S(1)}, f32[320,1,192]{0,2,1:T(8,128)}, u32[]{:S(2)}) copy-start(f32[320,1,192]{0,2,1:T(8,128)} %copy-done.12) | copy-start | bytes 737284
  103.7 23.8 %copy-start.15 = (f32[320,1,192]{0,2,1:T(8,128)S(1)}, f32[320,1,192]{0,2,1:T(8,128)}, u32[]{:S(2)}) copy-start(f32[320,1,192]{0,2,1:T(8,128)} %copy-done.14) | copy-start | bytes 737284
  103.7 23.8 %copy-start.17 = (f32[320,1,192]{0,2,1:T(8,128)S(1)}, f32[320,1,192]{0,2,1:T(8,128)}, u32[]{:S(2)}) copy-start(f32[320,1,192]{0,2,1:T(8,128)} %copy-done.16) | copy-start | bytes 737284
  103.7 23.8 %copy-start.19 = (f32[320,1,192]{0,2,1:T(8,128)S(1)}, f32[320,1,192]{0,2,1:T(8,128)}, u32[]{:S(2)}) copy-start(f32[320,1,192]{0,2,1:T(8,128)} %copy-done.18) | copy-start | bytes 737284
  130.0 26.6 %copy-start.2 = (bf16[1,1,768,768]{3,2,1,0:T(8,128)(2,1)S(1)}, bf16[1,1,768,768]{3,2,1,0:T(8,128)(2,1)}, u32[]{:S(2)}) copy-start(bf16[1,1,768,768]{3,2,1,0:T(8,128)(2,1)} %param.9) | copy-start | bytes 3538948
  162.0 7.4 %collective-permute-start.12 = (f32[320,192]{0,1:T(8,128)S(1)}, f32[320,192]{0,1:T(8,128)S(1)}, u32[]{:S(2)}, u32[]{:S(2)}) collective-permute-start(f32[320,192]{0,1:T(8,128)S(1)} %get-tuple-element.37), channel_id=1, source_target_pairs={{0,4},{4,8},{8,12},{12,16},{16,20},{20,24},{24,28},{1,5},{5,9},{9,... | collective-permute-start | bytes 737288 | tf_op jit(solution)/shard_map/ppermute | solution.py:14
  164.3 8.9 %collective-permute-start.14 = (f32[320,192]{0,1:T(8,128)S(1)}, f32[320,192]{0,1:T(8,128)S(1)}, u32[]{:S(2)}, u32[]{:S(2)}) collective-permute-start(f32[320,192]{0,1:T(8,128)S(1)} %get-tuple-element.38), channel_id=1, source_target_pairs={{0,1},{1,2},{2,3},{4,5},{5,6},{6,7},{8,9},{9,10},{10,11},{12,13},{... | collective-permute-start | bytes 737288 | tf_op jit(solution)/shard_map/ppermute | solution.py:14
  166.9 14.6 %collective-permute-start.15 = (f32[320,192]{0,1:T(8,128)S(1)}, f32[320,192]{0,1:T(8,128)S(1)}, u32[]{:S(2)}, u32[]{:S(2)}) collective-permute-start(f32[320,192]{0,1:T(8,128)S(1)} %get-tuple-element.39), channel_id=1, source_target_pairs={{1,0},{2,1},{3,2},{5,4},{6,5},{7,6},{9,8},{10,9},{11,10},{13,12},{... | collective-permute-start | bytes 737288 | tf_op jit(solution)/shard_map/ppermute | solution.py:14
  168.2 13.3 %collective-permute-start.13 = (f32[320,192]{0,1:T(8,128)S(1)}, f32[320,192]{0,1:T(8,128)S(1)}, u32[]{:S(2)}, u32[]{:S(2)}) collective-permute-start(f32[320,192]{0,1:T(8,128)S(1)} %get-tuple-element.40), channel_id=1, source_target_pairs={{4,0},{8,4},{12,8},{16,12},{20,16},{24,20},{28,24},{5,1},{9,5},{13... | collective-permute-start | bytes 737288 | tf_op jit(solution)/shard_map/ppermute | solution.py:14
  183.7 11.2 %collective-permute-start.16 = (f32[320,192]{0,1:T(8,128)}, f32[320,192]{0,1:T(8,128)}, u32[]{:S(2)}, u32[]{:S(2)}) collective-permute-start(f32[320,192]{0,1:T(8,128)} %get-tuple-element.28), channel_id=1, source_target_pairs={{0,4},{4,8},{8,12},{12,16},{16,20},{20,24},{24,28},{1,5},{5,9},{9,... | collective-permute-start | bytes 737288 | tf_op jit(solution)/shard_map/ppermute | solution.py:14
  185.7 9.2 %collective-permute-start.18 = (f32[320,192]{0,1:T(8,128)}, f32[320,192]{0,1:T(8,128)}, u32[]{:S(2)}, u32[]{:S(2)}) collective-permute-start(f32[320,192]{0,1:T(8,128)} %get-tuple-element.29), channel_id=1, source_target_pairs={{0,1},{1,2},{2,3},{4,5},{5,6},{6,7},{8,9},{9,10},{10,11},{12,13},{... | collective-permute-start | bytes 737288 | tf_op jit(solution)/shard_map/ppermute | solution.py:14
  189.8 12.1 %collective-permute-start.19 = (f32[320,192]{0,1:T(8,128)}, f32[320,192]{0,1:T(8,128)}, u32[]{:S(2)}, u32[]{:S(2)}) collective-permute-start(f32[320,192]{0,1:T(8,128)} %get-tuple-element.30), channel_id=1, source_target_pairs={{1,0},{2,1},{3,2},{5,4},{6,5},{7,6},{9,8},{10,9},{11,10},{13,12},{... | collective-permute-start | bytes 737288 | tf_op jit(solution)/shard_map/ppermute | solution.py:14
  191.1 10.8 %collective-permute-start.17 = (f32[320,192]{0,1:T(8,128)}, f32[320,192]{0,1:T(8,128)}, u32[]{:S(2)}, u32[]{:S(2)}) collective-permute-start(f32[320,192]{0,1:T(8,128)} %get-tuple-element.31), channel_id=1, source_target_pairs={{4,0},{8,4},{12,8},{16,12},{20,16},{24,20},{28,24},{5,1},{9,5},{13... | collective-permute-start | bytes 737288 | tf_op jit(solution)/shard_map/ppermute | solution.py:14
  203.7 22.4 %copy-start.41 = (f32[320]{0:T(512)S(1)}, f32[320]{0:T(512)}, u32[]{:S(2)}) copy-start(f32[320]{0:T(512)} %copy-done.40) | copy-start | bytes 3844
  203.7 22.3 %copy-start.43 = (f32[320]{0:T(512)S(1)}, f32[320]{0:T(512)}, u32[]{:S(2)}) copy-start(f32[320]{0:T(512)} %copy-done.42) | copy-start | bytes 3844
  203.7 22.4 %copy-start.3 = (f32[1,1,320,768]{3,2,1,0:T(8,128)S(1)}, f32[1,1,320,768]{3,2,1,0:T(8,128)}, u32[]{:S(2)}) copy-start(f32[1,1,320,768]{3,2,1,0:T(8,128)} %copy.29) | copy-start | bytes 2949124
  203.7 22.4 %copy-start.36 = (f32[320]{0:T(512)S(1)}, f32[320]{0:T(512)}, u32[]{:S(2)}) copy-start(f32[320]{0:T(512)} %copy-done.35) | copy-start | bytes 3844
  (35 other events, 125.3 us)
